TPU v7x, 256 devices: a whole 4x4x8 slice. The times are simulated.
256 devices in a mesh: row: 32 (over y, z), col: 8 (over x, core).
Axes of the slice: x: 4, y: 4, z: 8, core: 2. Of those that a mesh axis runs over, the one named last changes fastest.
Arguments:
- trail_adjoint: float32 [24576, 24576], P('row', 'col'), may hold values from -3 to 3
- panel: float32 [24576, 256], P(('row', 'col')), may hold values from -0.0390625 to 0.0390625
- panel_adjoint: float32 [24576, 256], P(('row', 'col')), may hold values from -6 to 6
- diag_factor: float32 [256, 256], replicated, as said below
- diag_inverse: float32 [256, 256], replicated, as said below
- diag_adjoint: float32 [256, 256], replicated, may hold values from -6 to 6
Outputs:
- panel_grad: float32 [24576, 256], P(('row', 'col'))
- diag_grad: float32 [256, 256], replicated
Inputs may be any that keep to these rules, and one draw needn't show every extreme that they name: diag_factor is lower triangular with a diagonal between 1 and 2, and diag_inverse is its inverse. diag_factor is lower triangular with a diagonal between 1 and 2.
All inputs are finite; a program needn't handle non-finite values.
Results may differ from a plain program's by a relative error of at most 0.000057.
Values sent between devices are 32-bit elements; how exact they have to be, the bound alone decides.
A program may use at most 128 MiB of HBM per device.

v0:
```python
import jax
import jax.numpy as jnp
from jax import lax
from jax.sharding import PartitionSpec as P


def lower_half(matrix):
    return jnp.tril(matrix) - 0.5 * jnp.diag(jnp.diag(matrix))


def on_device(trail_adjoint, panel, panel_adjoint, diag_factor, diag_inverse, diag_adjoint):
    highest = lax.Precision.HIGHEST
    col_place = lax.axis_index("col")
    trail_width = trail_adjoint.shape[1]
    row_block = lax.all_gather(panel, "col", axis=0, tiled=True)
    full_panel = lax.all_gather(row_block, "row", axis=0, tiled=True)
    column_panel = lax.dynamic_slice_in_dim(full_panel, col_place * trail_width, trail_width, 0)
    image = lax.psum_scatter(
        jnp.dot(trail_adjoint, column_panel, precision=highest, preferred_element_type=jnp.float32),
        "col",
        scatter_dimension=0,
        tiled=True,
    )
    updated = panel_adjoint - 2.0 * image
    panel_grad = jnp.dot(
        updated, diag_inverse, precision=highest, preferred_element_type=jnp.float32
    )
    local_gram = jnp.dot(panel_grad.T, panel, precision=highest, preferred_element_type=jnp.float32)
    gram = lax.psum(local_gram, ("row", "col"))
    corner = diag_adjoint - gram
    inner = lower_half(
        jnp.dot(diag_factor.T, corner, precision=highest, preferred_element_type=jnp.float32)
    )
    left_part = jnp.dot(
        diag_inverse.T, inner, precision=highest, preferred_element_type=jnp.float32
    )
    diag_grad = lower_half(
        jnp.dot(left_part, diag_inverse, precision=highest, preferred_element_type=jnp.float32)
    )
    return (panel_grad, diag_grad)


def solution(mesh):
    in_specs = (P("row", "col"), P(("row", "col"), None), P(("row", "col"), None), P(), P(), P())
    out_specs = (P(("row", "col"), None), P())
    return jax.shard_map(
        on_device, mesh=mesh, in_specs=in_specs, out_specs=out_specs, check_vma=False
    )
```

profile of v0, /device:TPU:2, one launch (start us, length us, event | category | flops | bytes accessed | tf_op | source)
XLA Modules:
  0.0 522.4 jit_solution(10304371956958443014)
XLA Ops:
  7.2 0.0 copy-start
  7.2 0.0 copy-start.1
  7.2 0.0 copy-start.5
  7.2 0.0 copy-start.3
  7.2 0.0 copy-start.4
  7.2 0.0 all-gather.2.cloned.1.call-start
  7.3 14.9 %all_gather.6 = f32[768,256]{1,0:T(8,128)} all-gather(f32[96,256]{1,0:T(8,128)} %param.7), channel_id=1, replica_groups=mesh['row'=32,'col'=8] {'col'}, dimensions={0}, use_global_device_ids=true | all-gather | bytes 884736 | tf_op jit(solution)/shard_map/all_gather | solution.py:15
  22.1 0.0 all-gather.2.cloned.1.call-update
  22.2 0.0 reduce-scatter.2.cloned.1.call-start
  22.2 186.5 %all-gather.2.cloned.1.call-done = f32[24576,256]{1,0:T(8,128)} async-done(((f32[768,256]{1,0:T(8,128)}), f32[24576,256]{1,0:T(8,128)}) %all-gather.2.cloned.1.call-update) | async-done | bytes 25165840 | tf_op jit(solution)/shard_map/all_gather | solution.py:16
  208.7 11.5 %fusion.2 = f32[768,256]{1,0:T(8,128)} fusion(f32[768,3072]{1,0:T(8,128)} %param.6, f32[24576,256]{1,0:T(8,128)} %all-gather.2.cloned.1.call-done, s32[]{:T(128)S(6)} %select_n.26), kind=kOutput, calls=%fused_computation.4 | convolution fusion | flops 7247757312 | bytes 13369348 | tf_op jit(solution)/shard_map/dot_general | solution.py:19
  220.2 0.0 reduce-scatter.2.cloned.1.call-update
  220.3 0.0 all-reduce.2.cloned.1.call-start
  220.3 28.0 %reduce-scatter.2.cloned.1.call-done = f32[96,256]{1,0:T(8,128)} async-done(((f32[768,256]{1,0:T(8,128)}), f32[96,256]{1,0:T(8,128)}) %reduce-scatter.2.cloned.1.call-update) | async-done | bytes 98320 | tf_op jit(solution)/shard_map/reduce_scatter | solution.py:18
  248.3 0.0 copy-done
  248.3 0.0 copy-done.5
  248.3 1.2 fusion.14
  249.5 0.0 copy-done.1
  249.5 0.0 copy-start.2
  249.5 1.1 fusion.22
  250.6 0.0 all-reduce.2.cloned.1.call-update
  250.6 256.9 %all-reduce.2.cloned.1.call-done = f32[256,256]{1,0:T(8,128)} async-done(((f32[256,256]{1,0:T(8,128)}), f32[256,256]{1,0:T(8,128)}) %all-reduce.2.cloned.1.call-update) | async-done | bytes 262160 | tf_op jit(solution)/shard_map/psum | solution.py:29
  507.6 0.0 copy-done.3
  507.6 0.0 copy-done.4
  507.6 1.5 convolution_bitcast_fusion
  509.2 2.4 gather_fusion
  511.5 0.4 fusion.5
  511.9 0.6 fusion.23
  512.5 0.1 copy.10
  512.7 2.3 gather_fusion.1
  515.1 0.8 copy.11
  515.9 0.0 copy-done.2
  (2 shorter events, 0.0 us)
Async XLA Ops:
  7.2 241.1 %copy-start = (f32[256,256]{1,0:T(8,128)S(1)}, f32[256,256]{1,0:T(8,128)}, u32[]{:S(2)}) copy-start(f32[256,256]{1,0:T(8,128)} %param.10) | copy-start | bytes 786436
  7.2 242.3 %copy-start.1 = (f32[96,256]{1,0:T(8,128)S(1)}, f32[96,256]{1,0:T(8,128)}, u32[]{:S(2)}) copy-start(f32[96,256]{1,0:T(8,128)} %param.7) | copy-start | bytes 294916
  7.2 241.1 %copy-start.5 = (f32[96,256]{1,0:T(8,128)S(1)}, f32[96,256]{1,0:T(8,128)}, u32[]{:S(2)}) copy-start(f32[96,256]{1,0:T(8,128)} %param.8) | copy-start | bytes 294916
  7.2 500.4 %copy-start.3 = (f32[256,256]{1,0:T(8,128)S(1)}, f32[256,256]{1,0:T(8,128)}, u32[]{:S(2)}) copy-start(f32[256,256]{1,0:T(8,128)} %param.9) | copy-start | bytes 786436
  7.2 500.4 %copy-start.4 = (f32[256,256]{1,0:T(8,128)S(1)}, f32[256,256]{1,0:T(8,128)}, u32[]{:S(2)}) copy-start(f32[256,256]{1,0:T(8,128)} %param.11) | copy-start | bytes 786436
  7.2 201.5 %all-gather.2.cloned.1.call-start = ((), (), s32[]{:S(2)}) async-start(), calls=%async_computation.1 | async-start | bytes 25952256 | tf_op jit(solution)/shard_map/all_gather | solution.py:16
  22.2 226.1 %reduce-scatter.2.cloned.1.call-start = ((), (), s32[]{:S(2)}) async-start(), calls=%async_computation.2 | async-start | bytes 884736 | tf_op jit(solution)/shard_map/reduce_scatter | solution.py:18
  220.3 287.3 %all-reduce.2.cloned.1.call-start = ((), (), s32[]{:S(2)}) async-start(), calls=%async_computation.3 | async-start | bytes 524288 | tf_op jit(solution)/shard_map/psum | solution.py:29
  249.5 266.4 %copy-start.2 = (f32[96,256]{1,0:T(8,128)}, f32[96,256]{1,0:T(8,128)S(1)}, u32[]{:S(2)}) copy-start(f32[96,256]{1,0:T(8,128)S(1)} %fusion.14) | copy-start | bytes 294916
Sparse Core Ops, SparseCore 0:
  22.3 186.4 all-gather.1
  220.4 27.8 reduce-scatter.1
  255.2 252.3 all-reduce.1
where the time goes:
time: 523 us; the launch traced here: 522 us
  waiting for transfers between devices  472 us (90%)
  matrix products  16.3 us (3%)
  blocking collectives  14.9 us (3%)
  between operations  13.9 us (3%)
  local copies, waits for them, and re-layouts  5.71 us (1%)
    psum x1, waiting for transfers between devices, on_device(): gram = lax.psum(local_gram, ('row', 'col'))  257 us
    all_gather x1, waiting for transfers between devices, on_device(): full_panel = lax.all_gather(row_block, 'row', axis=0, tiled=True)  187 us
    reduce_scatter x1, waiting for transfers between devices, on_device(): lax.psum_scatter(jnp.dot(trail_adjoint, column_panel, precision=highest,...  28 us
    all_gather x1, blocking collectives, on_device(): row_block = lax.all_gather(panel, 'col', axis=0, tiled=True)  14.9 us
    dot_general x1, matrix products, on_device(): jnp.dot(trail_adjoint, column_panel, precision=highest, preferred_element...  11.5 us
  transfers between devices with their start and end apart: 3, of which 3 were waited for; matrix products, arithmetic and copies ran while one was open for 0% of the time, Pallas kernels for 0%

commit v1 on v0

--- a/solution.py
+++ b/solution.py
@@ -26,7 +26,7 @@
         updated, diag_inverse, precision=highest, preferred_element_type=jnp.float32
     )
     local_gram = jnp.dot(panel_grad.T, panel, precision=highest, preferred_element_type=jnp.float32)
-    gram = lax.psum(local_gram, ("row", "col"))
+    gram = jnp.sum(lax.all_gather(local_gram, ("row", "col")), axis=0)
     corner = diag_adjoint - gram
     inner = lower_half(
         jnp.dot(diag_factor.T, corner, precision=highest, preferred_element_type=jnp.float32)

time: 523 us -> 504 us (0.964)
  waiting for transfers between devices: 472 us -> 431 us
  other arithmetic: 0.04 us -> 21.2 us
    psum x1 -> x0, waiting for transfers between devices: 257 us -> none  [on_device(): gram = lax.psum(local_gram, ('row', 'col'))]
    all_gather x0 -> x1, waiting for transfers between devices: none -> 217 us  [on_device(): gram = jnp.sum(lax.all_gather(local_gram, ('row', 'col')), axis=0)]
    reduce_sum x0 -> x1, other arithmetic: none -> 21.1 us  [on_device(): gram = jnp.sum(lax.all_gather(local_gram, ('row', 'col')), axis=0)]
where the time goes in v1:
time: 504 us; the launch traced here: 503 us
  waiting for transfers between devices  431 us (86%)
  other arithmetic  21.2 us (4%)
  matrix products  15.4 us (3%)
  blocking collectives  14.9 us (3%)
  between operations  13.9 us (3%)
  local copies, waits for them, and re-layouts  5.71 us (1%)
    all_gather x1, waiting for transfers between devices, on_device(): gram = jnp.sum(lax.all_gather(local_gram, ('row', 'col')), axis=0)  217 us
    all_gather x1, waiting for transfers between devices, on_device(): full_panel = lax.all_gather(row_block, 'row', axis=0, tiled=True)  187 us
    reduce_scatter x1, waiting for transfers between devices, on_device(): lax.psum_scatter(jnp.dot(trail_adjoint, column_panel, precision=highest,...  28 us
    reduce_sum x1, other arithmetic, on_device(): gram = jnp.sum(lax.all_gather(local_gram, ('row', 'col')), axis=0)  21.1 us
    all_gather x1, blocking collectives, on_device(): row_block = lax.all_gather(panel, 'col', axis=0, tiled=True)  14.9 us
    dot_general x1, matrix products, on_device(): jnp.dot(trail_adjoint, column_panel, precision=highest, preferred_element...  11.5 us
  transfers between devices with their start and end apart: 3, of which 3 were waited for; matrix products, arithmetic and copies ran while one was open for 0% of the time, Pallas kernels for 0%

profile of v1, /device:TPU:2, one launch (start us, length us, event | category | flops | bytes accessed | tf_op | source)
XLA Modules:
  0.0 502.6 jit_solution(10390380168168036105)
XLA Ops:
  7.2 0.0 copy-start
  7.2 0.0 copy-start.1
  7.2 0.0 copy-start.5
  7.2 0.0 all-gather.4.cloned.1.call-start
  7.2 14.9 %all_gather.12 = f32[768,256]{1,0:T(8,128)} all-gather(f32[96,256]{1,0:T(8,128)} %param.7), channel_id=1, replica_groups=mesh['row'=32,'col'=8] {'col'}, dimensions={0}, use_global_device_ids=true | all-gather | bytes 884736 | tf_op jit(solution)/shard_map/all_gather | solution.py:15
  22.1 0.0 all-gather.4.cloned.1.call-update
  22.1 0.0 reduce-scatter.2.cloned.1.call-start
  22.2 186.5 %all-gather.4.cloned.1.call-done = f32[24576,256]{1,0:T(8,128)} async-done(((f32[768,256]{1,0:T(8,128)}), f32[24576,256]{1,0:T(8,128)}) %all-gather.4.cloned.1.call-update) | async-done | bytes 25165840 | tf_op jit(solution)/shard_map/all_gather | solution.py:16
  208.7 11.5 %fusion.2 = f32[768,256]{1,0:T(8,128)} fusion(f32[768,3072]{1,0:T(8,128)} %param.6, f32[24576,256]{1,0:T(8,128)} %all-gather.4.cloned.1.call-done, s32[]{:T(128)S(6)} %select_n.26), kind=kOutput, calls=%fused_computation.4 | convolution fusion | flops 7247757312 | bytes 13369348 | tf_op jit(solution)/shard_map/dot_general | solution.py:19
  220.2 0.0 reduce-scatter.2.cloned.1.call-update
  220.2 0.0 all-gather.6.cloned.1.call-start
  220.3 28.0 %reduce-scatter.2.cloned.1.call-done = f32[96,256]{1,0:T(8,128)} async-done(((f32[768,256]{1,0:T(8,128)}), f32[96,256]{1,0:T(8,128)}) %reduce-scatter.2.cloned.1.call-update) | async-done | bytes 98320 | tf_op jit(solution)/shard_map/reduce_scatter | solution.py:18
  248.3 0.0 copy-done
  248.3 0.0 copy-done.5
  248.3 1.2 fusion.14
  249.4 0.0 copy-done.1
  249.5 0.0 copy-start.2
  249.5 1.1 fusion.22
  250.6 0.0 all-gather.6.cloned.1.call-update
  250.6 216.9 %all-gather.6.cloned.1.call-done = f32[65536,256]{1,0:T(8,128)} async-done(((f32[256,256]{1,0:T(8,128)}), f32[65536,256]{1,0:T(8,128)}) %all-gather.6.cloned.1.call-update) | async-done | bytes 67108880 | tf_op jit(solution)/shard_map/all_gather | solution.py:29
  467.5 0.0 copy-start.3
  467.5 0.0 copy-start.4
  467.5 21.1 %reduce_sum.9 = f32[256,256]{1,0:T(8,128)S(1)} reduce(f32[256,256,256]{2,1,0:T(8,128)} %bitcast.1, f32[]{:T(128)} %constant.29.clone.1), dimensions={0}, to_apply=%region_1.0 | reduce | flops 16711680 | bytes 67371008 | tf_op jit(solution)/shard_map/reduce_sum | solution.py:29
  488.7 0.0 copy-done.2
  488.7 0.0 copy-done.3
  488.7 0.0 copy-done.4
  488.7 0.6 convolution_bitcast_fusion
  489.3 2.4 gather_fusion
  491.7 0.4 fusion.5
  492.1 0.6 fusion.23
  492.7 2.3 gather_fusion.1
  495.0 0.1 copy.10
  495.2 0.8 copy.11
  (2 shorter events, 0.0 us)
Async XLA Ops:
  7.2 241.1 %copy-start = (f32[256,256]{1,0:T(8,128)S(1)}, f32[256,256]{1,0:T(8,128)}, u32[]{:S(2)}) copy-start(f32[256,256]{1,0:T(8,128)} %param.10) | copy-start | bytes 786436
  7.2 242.3 %copy-start.1 = (f32[96,256]{1,0:T(8,128)S(1)}, f32[96,256]{1,0:T(8,128)}, u32[]{:S(2)}) copy-start(f32[96,256]{1,0:T(8,128)} %param.7) | copy-start | bytes 294916
  7.2 241.1 %copy-start.5 = (f32[96,256]{1,0:T(8,128)S(1)}, f32[96,256]{1,0:T(8,128)}, u32[]{:S(2)}) copy-start(f32[96,256]{1,0:T(8,128)} %param.8) | copy-start | bytes 294916
  7.2 201.5 %all-gather.4.cloned.1.call-start = ((), (), s32[]{:S(2)}) async-start(), calls=%async_computation.1 | async-start | bytes 25952256 | tf_op jit(solution)/shard_map/all_gather | solution.py:16
  22.1 226.1 %reduce-scatter.2.cloned.1.call-start = ((), (), s32[]{:S(2)}) async-start(), calls=%async_computation.2 | async-start | bytes 884736 | tf_op jit(solution)/shard_map/reduce_scatter | solution.py:18
  220.2 247.3 %all-gather.6.cloned.1.call-start = ((), (), s32[]{:S(2)}) async-start(), calls=%async_computation.3 | async-start | bytes 67371008 | tf_op jit(solution)/shard_map/all_gather | solution.py:29
  249.5 239.2 %copy-start.2 = (f32[96,256]{1,0:T(8,128)}, f32[96,256]{1,0:T(8,128)S(1)}, u32[]{:S(2)}) copy-start(f32[96,256]{1,0:T(8,128)S(1)} %fusion.14) | copy-start | bytes 294916
  467.5 21.1 %copy-start.3 = (f32[256,256]{1,0:T(8,128)S(1)}, f32[256,256]{1,0:T(8,128)}, u32[]{:S(2)}) copy-start(f32[256,256]{1,0:T(8,128)} %param.9) | copy-start | bytes 786436
  467.5 21.2 %copy-start.4 = (f32[256,256]{1,0:T(8,128)S(1)}, f32[256,256]{1,0:T(8,128)}, u32[]{:S(2)}) copy-start(f32[256,256]{1,0:T(8,128)} %param.11) | copy-start | bytes 786436
Sparse Core Ops, SparseCore 0:
  22.3 186.4 all-gather.3
  220.4 27.8 reduce-scatter.1
  253.0 214.4 all-gather.5
